TPU v7x, 256 devices: a whole 4x4x8 slice. The times are simulated.
256 devices in a mesh: grp: 8 (over y, core), sub: 32 (over x, z).
Axes of the slice: x: 4, y: 4, z: 8, core: 2. Of those that a mesh axis runs over, the one named last changes fastest.
Arguments:
- right_side: float32 [65536, 2048], P(('grp', 'sub'))
- schur: bfloat16 [131072, 512], P(('grp', 'sub'))
- inv_factor: bfloat16 [131072, 512], P(('grp', 'sub'))
- coarse_inverse: float32 [2048, 256], P('grp')
- primal_index: int32 [256, 8], P(('grp', 'sub')), may hold values from 0 to 255
- phase: int32 [65536], P(('grp', 'sub')), may hold values from 0 to 3
- phase_coef: float32 [4], replicated, may hold values from 0.5 to 4
Outputs:
- solution: float32 [65536, 2048], P(('grp', 'sub'))
- residual: float32 [65536, 2048], P(('grp', 'sub'))
All inputs are finite; a program needn't handle non-finite values.
Results may differ from a plain program's by a relative error of at most 0.0056.
Values may be sent and summed in bfloat16 or wider, within the bound.
A program may use at most 64 MiB of HBM per device.

v0:
```python
import jax
import jax.numpy as jnp
from jax import lax
from jax.sharding import PartitionSpec as P


def shifted(value, axis, steps):
    count = lax.axis_size(axis)
    pairs = [(source, (source + steps) % count) for source in range(count)]
    return lax.ppermute(value, axis, pairs)


def transposed(matrix, operand):
    return lax.dot_general(
        matrix, operand, (((0,), (0,)), ((), ())), preferred_element_type=jnp.float32
    )


def body(right_side, schur, inv_factor, coarse_inverse, primal_index, phase, phase_coef):
    highest = lax.Precision.HIGHEST
    face_rows = right_side.shape[0]
    columns = jnp.arange(face_rows, dtype=jnp.int32)
    onehot = (primal_index[0][:, None] == columns[None, :]).astype(jnp.float32)
    primal_count = onehot.shape[0]
    resid_b = right_side.astype(jnp.bfloat16)
    left_resid = shifted(resid_b, "sub", 1)
    local_resid = jnp.concatenate([left_resid, resid_b], axis=0)
    first = jnp.dot(inv_factor, local_resid, preferred_element_type=jnp.float32).astype(
        jnp.bfloat16
    )
    second = transposed(inv_factor, first).astype(jnp.bfloat16)
    upper = second[:face_rows]
    from_right = shifted(upper, "sub", -1)
    lower = second[face_rows:]
    local_part = lower.astype(jnp.float32) + from_right.astype(jnp.float32)
    own_primal = jnp.dot(onehot, right_side, precision=highest)
    position = lax.axis_index("sub")
    group_primal = lax.all_gather(own_primal, "sub", axis=0, tiled=True)
    my_rows = lax.dynamic_slice_in_dim(coarse_inverse, position * primal_count, primal_count, 0)
    solved = jnp.dot(my_rows, group_primal, precision=highest)
    summed = lax.psum(solved, "grp")
    correction = solved + summed / lax.axis_size("grp")
    scattered = lax.dot_general(onehot, correction, (((0,), (0,)), ((), ())), precision=highest)
    direction = 0.5 * local_part + scattered
    dir_b = direction.astype(jnp.bfloat16)
    rz_part = jnp.sum(right_side * direction, axis=0)
    left_dir = shifted(dir_b, "sub", 1)
    image = jnp.dot(
        schur, jnp.concatenate([left_dir, dir_b], axis=0), preferred_element_type=jnp.float32
    ).astype(jnp.bfloat16)
    image_up = image[:face_rows]
    image_right = shifted(image_up, "sub", -1)
    image_low = image[face_rows:]
    phase_table = (
        phase[:, None] == jnp.arange(phase_coef.shape[0], dtype=jnp.int32)[None, :]
    ).astype(jnp.float32)
    coef_rows = jnp.dot(phase_table, phase_coef, precision=highest)
    dir_f = dir_b.astype(jnp.float32)
    qvec = (
        image_low.astype(jnp.float32) + image_right.astype(jnp.float32) + coef_rows[:, None] * dir_f
    )
    pq_part = jnp.sum(dir_f * qvec, axis=0)
    rz_total, pq_total = lax.psum((rz_part, pq_part), ("grp", "sub"))
    alpha = rz_total / pq_total
    return (alpha * dir_f, right_side - alpha * qvec)


def solution(mesh):
    in_specs = (
        P(("grp", "sub"), None),
        P(("grp", "sub"), None),
        P(("grp", "sub"), None),
        P("grp", None),
        P(("grp", "sub"), None),
        P(("grp", "sub")),
        P(),
    )
    out_specs = (P(("grp", "sub"), None), P(("grp", "sub"), None))
    return jax.shard_map(body, mesh=mesh, in_specs=in_specs, out_specs=out_specs, check_vma=False)
```

profile of v0, /device:TPU:1, one launch (start us, length us, event | category | flops | bytes accessed | tf_op | source)
XLA Modules:
  0.0 310.6 jit_solution(18175832615231809562)
XLA Ops:
  7.2 0.0 copy-start
  7.2 0.0 copy-start.1
  7.2 0.0 all-gather.2.cloned.1.call-start
  7.2 3.2 %fusion.21 = f32[8,2048]{1,0:T(8,128)} fusion(f32[256,2048]{1,0:T(8,128)} %param.7, s32[8]{0:T(128)} %bitcast.16), kind=kOutput, calls=%fused_computation.30 | convolution fusion | flops 50333696 | bytes 2162720 | tf_op jit(solution)/shard_map/dot_general | solution.py:36
  10.4 0.0 all-gather.2.cloned.1.call-update
  10.4 0.0 all-reduce.3.cloned.1.call-start
  10.5 0.0 copy-done.1
  10.5 0.1 convert_element_type.39
  10.6 0.0 copy-start.6
  10.6 1.0 copy-done.6
  11.6 2.5 collective-permute-start
  14.1 30.4 %collective-permute-done = bf16[256,2048]{1,0:T(8,128)(2,1)} collective-permute-done((bf16[256,2048]{1,0:T(8,128)(2,1)S(1)}, bf16[256,2048]{1,0:T(8,128)(2,1)}, u32[]{:S(2)}, u32[]{:S(2)}) %collective-permute-start) | collective-permute-done | bytes 1048608 | tf_op jit(solution)/shard_map/ppermute | solution.py:10
  44.5 0.0 copy-done
  44.5 5.3 %fusion = bf16[512,2048]{1,0:T(8,128)(2,1)} fusion(bf16[512,512]{1,0:T(8,128)(2,1)S(1)} %copy-done, bf16[256,2048]{1,0:T(8,128)(2,1)} %copy-done.6, bf16[256,2048]{1,0:T(8,128)(2,1)} %collective-permute-done), kind=kOutput, calls=%fused_computation.6 | convolution fusion | flops 2153775104 | bytes 4718592 | tf_op jit(solution)/shard_map/dot_general | solution.py:14
  49.8 0.0 copy-start.7
  49.8 2.3 slice.17
  52.1 1.3 collective-permute-start.1
  53.4 39.7 %all-gather.2.cloned.1.call-done = f32[256,2048]{1,0:T(8,128)} async-done(((f32[8,2048]{1,0:T(8,128)}), f32[256,2048]{1,0:T(8,128)}) %all-gather.2.cloned.1.call-update) | async-done | bytes 2097168 | tf_op jit(solution)/shard_map/all_gather | solution.py:38
  93.1 3.3 %fusion.19 = f32[8,2048]{1,0:T(8,128)} fusion(f32[256,2048]{1,0:T(8,128)} %all-gather.2.cloned.1.call-done, f32[256,256]{1,0:T(8,128)} %param.10, s32[]{:T(128)S(6)} %select_n.3), kind=kOutput, calls=%fused_computation.27 | convolution fusion | flops 50331648 | bytes 2170884 | tf_op jit(solution)/shard_map/dot_general | solution.py:40
  96.4 0.0 all-reduce.3.cloned.1.call-update
  96.4 65.5 %all-reduce.3.cloned.1.call-done = f32[8,2048]{1,0:T(8,128)} async-done(((f32[8,2048]{1,0:T(8,128)}), f32[8,2048]{1,0:T(8,128)}) %all-reduce.3.cloned.1.call-update) | async-done | bytes 65552 | tf_op jit(solution)/shard_map/psum | solution.py:41
  161.9 0.0 copy-done.7
  161.9 0.0 copy-start.5
  162.0 2.1 fusion.15
  164.1 0.0 copy-start.8
  164.1 0.0 collective-permute-done.1
  164.1 0.0 copy-done.5
  164.1 1.9 multiply_reduce_fusion
  166.0 0.0 copy-start.2
  166.0 1.2 collective-permute-start.2
  167.2 24.4 %collective-permute-done.2 = bf16[256,2048]{1,0:T(8,128)(2,1)S(1)} collective-permute-done((bf16[256,2048]{1,0:T(8,128)(2,1)S(1)}, bf16[256,2048]{1,0:T(8,128)(2,1)S(1)}, u32[]{:S(2)}, u32[]{:S(2)}) %collective-permute-start.2) | collective-permute-done | bytes 1048608 | tf_op jit(solution)/shard_map/ppermute | solution.py:10
  191.7 0.0 copy-done.8
  191.7 1.3 fusion.1
  192.9 0.0 copy-start.3
  193.0 0.0 copy-start.9
  193.0 0.0 copy-start.10
  193.0 0.1 slice.19
  193.1 1.3 collective-permute-start.3
  194.3 0.0 copy-done.9
  194.3 0.0 copy-done.10
  194.4 0.2 fusion.13
  194.5 19.8 %collective-permute-done.3 = bf16[256,2048]{1,0:T(8,128)(2,1)S(1)} collective-permute-done((bf16[256,2048]{1,0:T(8,128)(2,1)S(1)}, bf16[256,2048]{1,0:T(8,128)(2,1)S(1)}, u32[]{:S(2)}, u32[]{:S(2)}) %collective-permute-start.3) | collective-permute-done | bytes 1048608 | tf_op jit(solution)/shard_map/ppermute | solution.py:10
  214.3 0.0 copy-start.4
  214.3 0.0 copy-done.2
  214.3 0.7 fusion.3
  215.0 0.0 copy-done.3
  215.0 0.3 copy-done.4
  215.3 83.7 %all-reduce = (f32[2048]{0:T(1024)S(1)}, f32[2048]{0:T(1024)S(1)}) all-reduce(f32[2048]{0:T(1024)S(1)} %get-tuple-element.4, f32[2048]{0:T(1024)S(1)} %fusion.3), channel_id=1, replica_groups=mesh['grp'=8,'sub'=32] {'grp','sub'}, use_global_device_ids=true, to_apply=%region_2.0 | all-reduce | flops 4096 | bytes 32768 | tf_op jit(solution)/shard_map/psum | solution.py:63
  299.0 4.8 %multiply_subtract_fusion = (f32[256,2048]{1,0:T(8,128)}, f32[256,2048]{1,0:T(8,128)}) fusion(f32[256,2048]{1,0:T(8,128)S(1)} %copy-done.1, bf16[256,2048]{1,0:T(8,128)(2,1)} %copy-done.2, bf16[256,2048]{1,0:T(8,128)(2,1)} %copy-done.4, f32[2048]{0:T(1024)S(1)} %div.11, f32[256]{0:T(256)S(1)} %bitcast.15, bf16[512,2048]{1,0:T(8,128)(2,1)} %copy-done.3), kind=kLoop, calls=%fused_computation.16 | loop fusion | flops 4718592 | bytes 9446400 | tf_op jit(solution)/shard_map/sub | solution.py:65
  (1 shorter events, 0.0 us)
Async XLA Ops:
  7.2 37.3 %copy-start = (bf16[512,512]{1,0:T(8,128)(2,1)S(1)}, bf16[512,512]{1,0:T(8,128)(2,1)}, u32[]{:S(2)}) copy-start(bf16[512,512]{1,0:T(8,128)(2,1)} %param.9) | copy-start | bytes 1572868
  7.2 3.3 %copy-start.1 = (f32[256,2048]{1,0:T(8,128)S(1)}, f32[256,2048]{1,0:T(8,128)}, u32[]{:S(2)}) copy-start(f32[256,2048]{1,0:T(8,128)} %param.7) | copy-start | bytes 6291460
  7.2 85.9 %all-gather.2.cloned.1.call-start = ((), (), s32[]{:S(2)}) async-start(), calls=%async_computation | async-start | bytes 2162688 | tf_op jit(solution)/shard_map/all_gather | solution.py:38
  10.4 151.5 %all-reduce.3.cloned.1.call-start = ((), (), s32[]{:S(2)}) async-start(), calls=%async_computation.1 | async-start | bytes 131072 | tf_op jit(solution)/shard_map/psum | solution.py:41
  10.6 1.0 copy-start.6
  11.6 32.9 %collective-permute-start = (bf16[256,2048]{1,0:T(8,128)(2,1)S(1)}, bf16[256,2048]{1,0:T(8,128)(2,1)}, u32[]{:S(2)}, u32[]{:S(2)}) collective-permute-start(bf16[256,2048]{1,0:T(8,128)(2,1)S(1)} %convert_element_type.39), channel_id=1, source_target_pairs={{0,1},{1,2},{2,3},{3,4},{4,5},{5,6},{6,7},{7,8},{8,9},{9,10},{10,1... | collective-permute-start | bytes 3145736 | tf_op jit(solution)/shard_map/ppermute | solution.py:10
  49.8 112.2 %copy-start.7 = (s32[1,8]{1,0:T(1,128)S(1)}, s32[1,8]{1,0:T(1,128)}, u32[]{:S(2)}) copy-start(s32[1,8]{1,0:T(1,128)} %param.11) | copy-start | bytes 100
  52.1 112.0 %collective-permute-start.1 = (bf16[256,2048]{1,0:T(8,128)(2,1)}, bf16[256,2048]{1,0:T(8,128)(2,1)}, u32[]{:S(2)}, u32[]{:S(2)}) collective-permute-start(bf16[256,2048]{1,0:T(8,128)(2,1)} %slice.17), channel_id=1, source_target_pairs={{0,31},{1,0},{2,1},{3,2},{4,3},{5,4},{6,5},{7,6},{8,7},{9,8},{10,9... | collective-permute-start | bytes 3145736 | tf_op jit(solution)/shard_map/ppermute | solution.py:10
  161.9 2.1 copy-start.5
  164.1 27.6 %copy-start.8 = (bf16[512,512]{1,0:T(8,128)(2,1)S(1)}, bf16[512,512]{1,0:T(8,128)(2,1)}, u32[]{:S(2)}) copy-start(bf16[512,512]{1,0:T(8,128)(2,1)} %param.8) | copy-start | bytes 1572868
  166.0 48.3 %copy-start.2 = (bf16[256,2048]{1,0:T(8,128)(2,1)}, bf16[256,2048]{1,0:T(8,128)(2,1)S(1)}, u32[]{:S(2)}) copy-start(bf16[256,2048]{1,0:T(8,128)(2,1)S(1)} %get-tuple-element.5) | copy-start | bytes 3145732
  166.0 25.7 %collective-permute-start.2 = (bf16[256,2048]{1,0:T(8,128)(2,1)S(1)}, bf16[256,2048]{1,0:T(8,128)(2,1)S(1)}, u32[]{:S(2)}, u32[]{:S(2)}) collective-permute-start(bf16[256,2048]{1,0:T(8,128)(2,1)S(1)} %get-tuple-element.5), channel_id=1, source_target_pairs={{0,1},{1,2},{2,3},{3,4},{4,5},{5,6},{6,7},{7,8},{8,9},{9,10},{10,1... | collective-permute-start | bytes 3145736 | tf_op jit(solution)/shard_map/ppermute | solution.py:10
  192.9 22.1 %copy-start.3 = (bf16[512,2048]{1,0:T(8,128)(2,1)}, bf16[512,2048]{1,0:T(8,128)(2,1)S(1)}, u32[]{:S(2)}) copy-start(bf16[512,2048]{1,0:T(8,128)(2,1)S(1)} %fusion.1) | copy-start | bytes 6291460
  193.0 1.4 copy-start.9
  193.0 1.4 copy-start.10
  193.1 21.2 %collective-permute-start.3 = (bf16[256,2048]{1,0:T(8,128)(2,1)S(1)}, bf16[256,2048]{1,0:T(8,128)(2,1)S(1)}, u32[]{:S(2)}, u32[]{:S(2)}) collective-permute-start(bf16[256,2048]{1,0:T(8,128)(2,1)S(1)} %slice.19), channel_id=1, source_target_pairs={{0,31},{1,0},{2,1},{3,2},{4,3},{5,4},{6,5},{7,6},{8,7},{9,8},{10,9... | collective-permute-start | bytes 3145736 | tf_op jit(solution)/shard_map/ppermute | solution.py:10
  214.3 1.0 copy-start.4
Sparse Core Ops, SparseCore 0:
  10.6 82.4 all-gather.1
  96.6 65.3 all-reduce.2
where the time goes:
time: 311 us
  waiting for transfers between devices  180 us (58%)
  blocking collectives  83.7 us (27%)
  matrix products  15.3 us (5%)
  between operations  14.2 us (5%)
  other arithmetic  7.52 us (2%)
  starting transfers between devices  6.3 us (2%)
  local copies, waits for them, and re-layouts  3.72 us (1%)
    psum x1, blocking collectives, body(): rz_total, pq_total = lax.psum((rz_part, pq_part), ('grp', 'sub'))  83.7 us
    ppermute x4, waiting for transfers between devices, shifted(): return lax.ppermute(value, axis, pairs)  74.7 us
    psum x1, waiting for transfers between devices, body(): summed = lax.psum(solved, 'grp')  65.5 us
    all_gather x1, waiting for transfers between devices, body(): group_primal = lax.all_gather(own_primal, 'sub', axis=0, tiled=True)  39.7 us
  transfers between devices with their start and end apart: 6, of which 5 were waited for; matrix products, arithmetic and copies ran while one was open for 4% of the time, Pallas kernels for 0%

commit v1 on v0

v1 whole, which is shorter than its diff:
```python
import jax
import jax.numpy as jnp
from jax import lax
from jax.experimental import pallas as pl
from jax.experimental.pallas import tpu as pltpu
from jax.sharding import PartitionSpec as P

MESH = pl.DeviceIdType.MESH
F32 = jnp.float32
BF16 = jnp.bfloat16
NX, NZ = 4, 8
WIDTH = 256
AHEAD = 2
LAG = 2


def kernel(
    idx_ref, coef_ref, phase_ref, rs_hbm, g_hbm, s_hbm, k_hbm,
    zb_out, q_out, alpha_out,
    rs, gm, gt, sm, km, xs, vs, vl, vr, zs, ys, yl, yr, onehot, coef_col, esplit,
    rc, xg, rr, hb, hr, ag, eb, e5, e6, ara, arb, arc,
    load_sem, mat_sem, shift_send, shift_recv, co_send, co_recv, ar_send, ar_recv,
):
    n_grp, n_sub = lax.axis_size("grp"), lax.axis_size("sub")
    g, s = lax.axis_index("grp"), lax.axis_index("sub")
    x, z = lax.div(s, NZ), lax.rem(s, NZ)
    half, block = lax.div(z, 4), lax.rem(z, 4)
    right, left = lax.rem(s + 1, n_sub), lax.rem(s + n_sub - 1, n_sub)
    rows = rs.shape[1]
    chunks, width = rs.shape[0], rs.shape[2]
    per = width // 128
    upper, lower = pl.ds(0, rows), pl.ds(rows, rows)

    def x_peer(d):
        p = lax.rem(x + d, NX)
        return p, {"sub": p * NZ + z}

    def z_peer(d):
        p = lax.rem(z + d, NZ)
        return p, {"sub": x * NZ + p}

    def g_peer(d):
        p = lax.rem(g + d, n_grp)
        return p, {"grp": p}

    def load(c):
        return pltpu.make_async_copy(
            rs_hbm.at[:, pl.ds(c * width, width)], rs.at[c], load_sem.at[c]
        )

    mats = [
        pltpu.make_async_copy(src, dst, mat_sem.at[i])
        for i, (src, dst) in enumerate([(g_hbm, gm), (k_hbm, km), (s_hbm, sm)])
    ]

    def signal(to):
        pl.semaphore_signal(
            pltpu.get_barrier_semaphore(), inc=1, device_id=to, device_id_type=MESH
        )

    def remote(src, dst, send, recv, to):
        return pltpu.make_async_remote_copy(
            src_ref=src, dst_ref=dst, send_sem=send, recv_sem=recv,
            device_id=to, device_id_type=MESH,
        )

    def shift(which, c):
        src, dst, to = (
            (xs.at[c, lower], xs.at[c, upper], right),
            (vs.at[c], vr.at[c], left),
            (zs.at[c, lower], zs.at[c, upper], right),
            (ys.at[c], yr.at[c], left),
        )[which]
        return remote(src, dst, shift_send.at[which, c], shift_recv.at[which, c], {"sub": to})

    for peer, count in ((x_peer, NX), (z_peer, NZ), (g_peer, n_grp)):
        for d in range(1, count):
            signal(peer(d)[1])
    signal({"sub": right})
    signal({"sub": left})
    for c in range(chunks):
        load(c).start()
    for m in mats:
        m.start()

    lane = lax.broadcasted_iota(jnp.int32, onehot.shape, 1)
    row = lax.broadcasted_iota(jnp.int32, onehot.shape, 0)
    want = jnp.full(onehot.shape, -1, jnp.int32)
    for k in range(8):
        want = jnp.where((lax.rem(lane, 8) == k) & (lane < 24), idx_ref[0, k], want)
    onehot[...] = (want == row).astype(F32).astype(BF16)
    coef_row = jnp.zeros(phase_ref.shape, F32)
    for p in range(4):
        coef_row = jnp.where(phase_ref[...] == p, coef_ref[p], coef_row)
    coef_col[...] = jnp.transpose(jnp.broadcast_to(coef_row, (128, rows)))

    for c in range(chunks):
        load(c).wait()
        xs[c, lower] = rs[c].astype(BF16)

    pl.semaphore_wait(
        pltpu.get_barrier_semaphore(), NX - 1 + NZ - 1 + n_grp - 1 + 2
    )

    for c in range(AHEAD):
        shift(0, c).start()

    lane8 = lax.broadcasted_iota(jnp.int32, (8, rows), 1)
    row8 = lax.broadcasted_iota(jnp.int32, (8, rows), 0)
    want8 = jnp.full((8, rows), -1, jnp.int32)
    for k in range(8):
        want8 = jnp.where(row8 == k, idx_ref[0, k], want8)
    pick = (want8 == lane8).astype(F32)
    for c in range(chunks):
        picked = jnp.dot(
            pick, rs[c], precision=lax.Precision.HIGHEST, preferred_element_type=F32
        )
        for i in range(per):
            cb = c * per + i
            rc[cb // 4, cb % 4] = picked[:, i * 128 : (i + 1) * 128]

    def exchange(stage, peer, count, src, dst, me, send=co_send, recv=co_recv):
        def out(d):
            p, to = peer(d)
            return remote(src(p), dst(me), send.at[stage, p], recv.at[stage, me], to)

        def arriving(d):
            p, to = peer(d)
            return remote(src(p), dst(p), send.at[stage, p], recv.at[stage, p], to)

        def start():
            for d in range(1, count):
                out(d).start()

        def wait():
            for d in range(1, count):
                arriving(d).wait_recv()

        def drain():
            for d in range(1, count):
                out(d).wait_send()

        return start, wait, drain

    st1 = exchange(0, x_peer, NX, lambda p: rc.at[p], lambda me: xg.at[:, me], x)
    st2 = exchange(1, z_peer, NZ, lambda p: xg.at[lax.rem(p, 4)], lambda me: rr.at[:, me], z)
    st3 = exchange(2, g_peer, n_grp, lambda p: hb.at[p], lambda me: hr.at[me], g)
    st4 = exchange(3, g_peer, n_grp, lambda p: ag.at[g], lambda me: ag.at[me], g)
    st5 = exchange(
        4, z_peer, NZ, lambda p: eb.at[:, p],
        lambda me: e5.at[pl.ds(lax.div(me, 4) * 2, 2), lax.rem(me, 4)], z,
    )
    st6 = exchange(5, x_peer, NX, lambda p: e5.at[p], lambda me: e6.at[pl.ds(me * 4, 4)], x)

    xg[:, x] = rc[x]
    st1[0]()

    mats[0].wait()
    gt[...] = jnp.transpose(gm[...])
    mats[1].wait()
    mats[2].wait()

    def to_owners():
        st1[1]()
        rr[:, z] = xg[block]
        st2[0]()

    def solve():
        st2[1]()
        mine = km[pl.ds(pl.multiple_of(half * 128, 128), 128), :]
        solved = jnp.dot(
            mine, rr[...].reshape(256, 128),
            precision=lax.Precision.HIGHEST, preferred_element_type=F32,
        )
        hb[...] = solved.reshape(hb.shape)
        hr[g] = hb[g]
        st3[0]()

    def mean():
        st3[1]()
        total = hr[0]
        for p in range(1, n_grp):
            total = total + hr[p]
        ag[g] = total / n_grp
        st4[0]()

    def back():
        st4[1]()
        eb[...] = (hb[...] + ag[...]).reshape(eb.shape)
        e5[pl.ds(half * 2, 2), block] = eb[:, z]
        st5[0]()

    def spread():
        st5[1]()
        e6[pl.ds(x * 4, 4)] = e5[x]
        st6[0]()

    events = {0: to_owners, 3: solve, 4: mean, 5: back, 7: spread}

    def first(c, _):
        shift(0, c).wait_recv()

        @pl.when(c + AHEAD < chunks)
        def _():
            shift(0, c + AHEAD).start()

        u = jnp.dot(gm[...], xs[c], preferred_element_type=F32).astype(BF16)
        v = jnp.dot(gt[...], u, preferred_element_type=F32).astype(BF16)
        vs[c] = v[:rows]
        shift(1, c).start()
        vl[c] = v[rows:]
        for at, event in events.items():
            pl.when(c == at)(event)
        return 0

    lax.fori_loop(0, chunks, first, 0)

    st6[1]()
    for cb in range(NX * 4):
        c, off = cb // per, (cb % per) * 128
        e = e6[cb]
        e1 = e.astype(BF16)
        rest = e - e1.astype(F32)
        e2 = rest.astype(BF16)
        e3 = (rest - e2.astype(F32)).astype(BF16)
        parts = [e1.astype(F32), e2.astype(F32), e3.astype(F32), jnp.zeros_like(e)]
        esplit[c, :, pl.ds(off, 128)] = jnp.concatenate(parts, axis=0).astype(BF16)

    coef = jnp.concatenate([coef_col[...]] * per, axis=1)

    def second(c):
        shift(1, c).wait_recv()
        scattered = jnp.dot(onehot[...], esplit[c], preferred_element_type=F32)
        direction = 0.5 * (vl[c].astype(F32) + vr[c].astype(F32)) + scattered
        zs[c, lower] = direction.astype(BF16)
        shift(2, c).start()
        ara[g, c, 0:1] = jnp.sum(rs[c] * direction, axis=0, keepdims=True)

    def third(c):
        shift(2, c).wait_recv()
        y = jnp.dot(sm[...], zs[c], preferred_element_type=F32).astype(BF16)
        ys[c] = y[:rows]
        shift(3, c).start()
        yl[c] = y[rows:]
        both = zs[c].astype(F32) * y.astype(F32)
        own = zs[c, lower].astype(F32)
        terms = both[:rows] + both[rows:] + coef * own * own
        ara[g, c, 1:2] = jnp.sum(terms, axis=0, keepdims=True)

    def fourth(c):
        shift(3, c).wait_recv()
        own = zs[c, lower]
        cols = pl.ds(pl.multiple_of(c * width, width), width)
        zb_out[:, cols] = own
        q_out[:, cols] = yl[c].astype(F32) + yr[c].astype(F32) + coef * own.astype(F32)

    for c in range(AHEAD):
        second(c)

    def rest(c, _):
        @pl.when(c + AHEAD < chunks)
        def _():
            second(c + AHEAD)

        third(c)

        @pl.when(c >= LAG)
        def _():
            fourth(c - LAG)

        return 0

    lax.fori_loop(0, chunks, rest, 0)

    sta = exchange(0, g_peer, n_grp, lambda p: ara.at[g], lambda me: ara.at[me], g, ar_send, ar_recv)
    stb = exchange(1, x_peer, NX, lambda p: arb.at[x], lambda me: arb.at[me], x, ar_send, ar_recv)
    stc = exchange(2, z_peer, NZ, lambda p: arc.at[z], lambda me: arc.at[me], z, ar_send, ar_recv)

    def total(buf, count):
        acc = buf[0]
        for p in range(1, count):
            acc = acc + buf[p]
        return acc

    sta[0]()
    for c in range(chunks - LAG, chunks - LAG + 1):
        fourth(c)
    sta[1]()
    arb[x] = total(ara, n_grp)
    stb[0]()
    for c in range(chunks - LAG + 1, chunks):
        fourth(c)
    stb[1]()
    arc[z] = total(arb, NX)
    stc[0]()
    stc[1]()
    sums = total(arc, NZ)
    for c in range(chunks):
        alpha_out[:, pl.ds(c * width, width)] = sums[c, 0:1] / sums[c, 1:2]

    for st in (st1, st2, st3, st4, st5, st6, sta, stb, stc):
        st[2]()

    def drain(c, _):
        for which in range(4):
            shift(which, c).wait_send()
        return 0

    lax.fori_loop(0, chunks, drain, 0)


def body(right_side, schur, inv_factor, coarse_inverse, primal_index, phase, phase_coef):
    rows, cols = right_side.shape
    n = cols // WIDTH
    n_grp = lax.axis_size("grp")
    smem = pl.BlockSpec(memory_space=pltpu.SMEM)
    vmem = pl.BlockSpec(memory_space=pltpu.VMEM)
    hbm = pl.BlockSpec(memory_space=pl.ANY)
    chunked = pltpu.VMEM((n, rows, WIDTH), BF16)
    stacked = pltpu.VMEM((n, 2 * rows, WIDTH), BF16)
    square = pltpu.VMEM(schur.shape, BF16)
    dma = pltpu.SemaphoreType.DMA
    zb, q, alpha = pl.pallas_call(
        kernel,
        out_shape=(
            jax.ShapeDtypeStruct((rows, cols), BF16),
            jax.ShapeDtypeStruct((rows, cols), F32),
            jax.ShapeDtypeStruct((1, cols), F32),
        ),
        in_specs=[smem, smem, vmem, hbm, hbm, hbm, hbm],
        out_specs=(vmem, vmem, vmem),
        scratch_shapes=[
            pltpu.VMEM((n, rows, WIDTH), F32),
            square, square, square,
            pltpu.VMEM(coarse_inverse.shape, F32),
            stacked, chunked, chunked, chunked, stacked, chunked, chunked, chunked,
            pltpu.VMEM((rows, 32), BF16),
            pltpu.VMEM((rows, 128), F32),
            pltpu.VMEM((n, 32, WIDTH), BF16),
            pltpu.VMEM((NX, 4, 8, 128), F32),
            pltpu.VMEM((4, NX, 8, 128), F32),
            pltpu.VMEM((NX, NZ, 8, 128), F32),
            pltpu.VMEM((n_grp, 16, 128), F32),
            pltpu.VMEM((n_grp, 16, 128), F32),
            pltpu.VMEM((n_grp, 16, 128), F32),
            pltpu.VMEM((2, NZ, 8, 128), F32),
            pltpu.VMEM((NX, 4, 8, 128), F32),
            pltpu.VMEM((NX * 4, 8, 128), F32),
            pltpu.VMEM((n_grp, n, 2, WIDTH), F32),
            pltpu.VMEM((NX, n, 2, WIDTH), F32),
            pltpu.VMEM((NZ, n, 2, WIDTH), F32),
            dma((n,)), dma((3,)), dma((4, n)), dma((4, n)),
            dma((6, 8)), dma((6, 8)), dma((3, 8)), dma((3, 8)),
        ],
        compiler_params=pltpu.CompilerParams(
            collective_id=0, has_side_effects=True, vmem_limit_bytes=56 * 2**20
        ),
    )(
        primal_index, phase_coef, phase.reshape(1, rows),
        right_side, inv_factor, schur, coarse_inverse,
    )
    return alpha * zb.astype(F32), right_side - alpha * q


def solution(mesh):
    in_specs = (
        P(("grp", "sub"), None),
        P(("grp", "sub"), None),
        P(("grp", "sub"), None),
        P("grp", None),
        P(("grp", "sub"), None),
        P(("grp", "sub")),
        P(),
    )
    out_specs = (P(("grp", "sub"), None), P(("grp", "sub"), None))
    return jax.shard_map(body, mesh=mesh, in_specs=in_specs, out_specs=out_specs, check_vma=False)
```

time: 311 us -> 95.7 us (0.31)
  waiting for transfers between devices: 180 us -> 0 us
  Pallas kernels: 0 us -> 90.5 us
  blocking collectives: 83.7 us -> 0 us
  matrix products: 15.3 us -> 0 us
  between operations: 14.2 us -> 0.66 us
  starting transfers between devices: 6.3 us -> 0 us
  local copies, waits for them, and re-layouts: 3.72 us -> 0.01 us
    pallas_call x0 -> x1, Pallas kernels: none -> 90.5 us  [body(): pl.pallas_call(kernel, out_shape=(jax.ShapeDtypeStruct((rows, cols), BF16...]
    psum x1 -> x0, blocking collectives: 83.7 us -> none  [body(): rz_total, pq_total = lax.psum((rz_part, pq_part), ('grp', 'sub'))]
    ppermute x4 -> x0, waiting for transfers between devices: 74.7 us -> none  [shifted(): return lax.ppermute(value, axis, pairs)]
    psum x1 -> x0, waiting for transfers between devices: 65.5 us -> none  [body(): summed = lax.psum(solved, 'grp')]
    all_gather x1 -> x0, waiting for transfers between devices: 39.7 us -> none  [body(): group_primal = lax.all_gather(own_primal, 'sub', axis=0, tiled=True)]
    dot_general x6 -> x0, matrix products: 15.3 us -> none  [the longest x1 5.26 us: transposed(): lax.dot_general(matrix, operand, (((0,), (0,)), ((), ())), preferred_elem...]
    ppermute x4 -> x0, starting transfers between devices: 6.22 us -> none  [shifted(): return lax.ppermute(value, axis, pairs)]
  transfers between devices with their start and end apart: 6 -> 0, of which waited for: 5 -> 0; matrix products, arithmetic and copies ran while one was open for 4% -> 0% of each run, Pallas kernels for 0% -> 0%
where the time goes in v1:
time: 95.7 us; the launch traced here: 95.6 us
  Pallas kernels  90.5 us (95%)
  other arithmetic  4.45 us (5%)
    pallas_call x1, Pallas kernels, body(): pl.pallas_call(kernel, out_shape=(jax.ShapeDtypeStruct((rows, cols), BF16...  90.5 us
    sub x1, other arithmetic, body(): return (alpha * zb.astype(F32), right_side - alpha * q)  4.45 us

profile of v1, /device:TPU:1, one launch (start us, length us, event | category | flops | bytes accessed | tf_op | source)
XLA Modules:
  0.0 95.6 jit_solution(16274375144593926951)
XLA Ops:
  0.6 0.0 copy-start
  0.6 90.5 %shard_map.86 = (bf16[256,2048]{1,0:T(8,128)(2,1)}, f32[256,2048]{1,0:T(8,128)}, f32[1,2048]{1,0:T(1,128)}) custom-call(s32[1,8]{1,0:T(1,128)} %idx_ref.1, f32[4]{0:T(128)} %coef_ref.1, s32[1,256]{1,0:T(1,128)} %bitcast.3, f32[256,2048]{1,0:T(8,128)} %rs_hbm.1, bf16[512,512]{1,0:T(8,128)(2,1)} %g_hbm.1, bf16[512,512]{1,0:T(8,128)(2,1)} %s_hbm.1, ...), custom_call_target="tpu_custom_call" | custom-call | tf_op jit(solution)/shard_map/pallas_call | solution.py:323
  91.1 0.0 copy-done
  91.1 4.5 %multiply_subtract_fusion = (f32[256,2048]{1,0:T(8,128)}, f32[256,2048]{1,0:T(8,128)}) fusion(f32[256,2048]{1,0:T(8,128)S(1)} %copy-done, f32[256,2048]{1,0:T(8,128)} %get-tuple-element.7, f32[2048]{0:T(1024)} %bitcast.2, bf16[256,2048]{1,0:T(8,128)(2,1)} %get-tuple-element.6), kind=kLoop, calls=%fused_computation | loop fusion | flops 2097152 | bytes 9445376 | tf_op jit(solution)/shard_map/sub | solution.py:362
Async XLA Ops:
  0.6 90.5 %copy-start = (f32[256,2048]{1,0:T(8,128)S(1)}, f32[256,2048]{1,0:T(8,128)}, u32[]{:S(2)}) copy-start(f32[256,2048]{1,0:T(8,128)} %rs_hbm.1) | copy-start | bytes 6291460
